TPU v7x, 32 devices: a whole 2x2x4 slice. The times are simulated.
32 devices in a mesh: shard: 16 (over z, x, core), ctx: 2 (over y).
Axes of the slice: x: 2, y: 2, z: 4, core: 2. Of those that a mesh axis runs over, the one named last changes fastest.
Arguments:
- tokens: bfloat16 [8192, 576], P(('shard', 'ctx')), may hold values from -6 to 6
- cotangent: bfloat16 [8192, 576], P(('shard', 'ctx')), may hold values from -6 to 6
- seq_lengths: int32 [16], P('shard'), may hold values from 64 to 512, as said below
- attn_params: float32 [885888], P('shard')
- attn_first: float32 [885888], P('shard'), may hold values from -6 to 6
- attn_second: float32 [885888], P('shard'), may hold values from 1 to 100
- ffn_params: float32 [2654208], P('shard')
- ffn_first: float32 [2654208], P('shard'), may hold values from -6 to 6
- ffn_second: float32 [2654208], P('shard'), may hold values from 1 to 100
Outputs:
- outputs: bfloat16 [8192, 576], P(('shard', 'ctx'))
- grad_tokens: bfloat16 [8192, 576], P(('shard', 'ctx'))
- attn_grad: float32 [885888], P('shard')
- ffn_grad: float32 [2654208], P('shard')
- attn_new: float32 [885888], P('shard')
- attn_first_new: float32 [885888], P('shard')
- attn_second_new: float32 [885888], P('shard')
- ffn_new: float32 [2654208], P('shard')
- ffn_first_new: float32 [2654208], P('shard')
- ffn_second_new: float32 [2654208], P('shard')
Inputs may be any that keep to these rules, and one draw needn't show every extreme that they name: `seq_lengths`: in every draw some sequence fills all 512 slots.
All inputs are finite; a program needn't handle non-finite values.
Results may differ from a plain program's by a relative error of at most 0.01.
The roundings to bfloat16 on the way count: a program that leaves them out, or rounds other values in their place, can miss the bound.
Values may be sent and summed in bfloat16 or wider, within the bound.
A program may use at most 128 MiB of HBM per device.

v0:
```python
import math
import jax
import jax.numpy as jnp
from jax import lax
from jax.sharding import PartitionSpec as P

MODEL_WIDTH = 576
QUERY_HEADS = 9
KEY_VALUE_HEADS = 3
HEAD_SIZE = 64
FF = 1536
ADAM_STEP = 3
rms_eps = 1e-05
rope_base = 100000.0
beta_one = 0.9
beta_two = 0.95
learn_rate = 0.02
decay_rate = 0.1
adam_eps = 1e-08
masked_score = -1e30


def split_flattened(flattened, shapes):
    pieces = []
    offset = 0
    for shape in shapes:
        width = 1
        for extent in shape:
            width = width * extent
        pieces.append(flattened[offset : offset + width].reshape(shape))
        offset = offset + width
    return pieces


def split_attention(flattened):
    return split_flattened(
        flattened,
        (
            (MODEL_WIDTH, QUERY_HEADS * HEAD_SIZE),
            (MODEL_WIDTH, KEY_VALUE_HEADS * HEAD_SIZE),
            (MODEL_WIDTH, KEY_VALUE_HEADS * HEAD_SIZE),
            (QUERY_HEADS * HEAD_SIZE, MODEL_WIDTH),
            (MODEL_WIDTH,),
            (MODEL_WIDTH,),
        ),
    )


def split_feedforward(flattened):
    return split_flattened(flattened, ((MODEL_WIDTH, FF), (MODEL_WIDTH, FF), (FF, MODEL_WIDTH)))


def rope_tables(positions):
    index = jnp.arange(HEAD_SIZE // 2).astype(jnp.float32)
    inverse = jnp.exp(index * (-2.0 * math.log(rope_base) / HEAD_SIZE))
    angles = positions.astype(jnp.float32)[:, None] * inverse[None, :]
    angles = jnp.concatenate([angles, angles], axis=1)
    return (jnp.cos(angles), jnp.sin(angles))


def apply_rotation(values, cosine_table, sine_table):
    half = values.shape[-1] // 2
    turned = jnp.concatenate([-values[..., half:], values[..., :half]], axis=-1)
    return values * cosine_table[:, None, :] + turned * sine_table[:, None, :]


def reverse_rotation(grads, cosine_table, sine_table):
    half = grads.shape[-1] // 2
    weighted = grads * sine_table[:, None, :]
    turned = jnp.concatenate([weighted[..., half:], -weighted[..., :half]], axis=-1)
    return grads * cosine_table[:, None, :] + turned


def norm_rows(values, gain):
    mean_sq = jnp.mean(values * values, axis=-1, keepdims=True)
    inverse = lax.rsqrt(mean_sq + rms_eps)
    scaled = values * inverse
    return (scaled, inverse, (scaled * gain).astype(jnp.bfloat16))


def norm_back(grad_normed, scaled, inverse, gain):
    grad_scaled = grad_normed * gain
    grad_gain = jnp.sum(grad_normed * scaled, axis=0)
    inner = jnp.mean(grad_scaled * scaled, axis=-1, keepdims=True)
    return (inverse * (grad_scaled - scaled * inner), grad_gain)


def attend(query_rows, keys, values, mask):
    row_entries = query_rows.shape[0]
    scale = 1.0 / math.sqrt(HEAD_SIZE)
    grouped_heads = query_rows.reshape(
        row_entries, KEY_VALUE_HEADS, QUERY_HEADS // KEY_VALUE_HEADS, HEAD_SIZE
    )
    scores = (
        jnp.einsum("tkgd,skd->kgts", grouped_heads, keys, preferred_element_type=jnp.float32)
        * scale
    )
    scores = jnp.where(mask[None, None], scores, masked_score)
    top = jnp.max(scores, axis=-1, keepdims=True)
    total = jnp.sum(jnp.exp(scores - top), axis=-1, keepdims=True)
    log_total = top + jnp.log(total)
    probs = jnp.exp(scores - log_total).astype(jnp.bfloat16)
    mixture = jnp.einsum("kgts,skd->tkgd", probs, values, preferred_element_type=jnp.float32)
    return (mixture.reshape(row_entries, QUERY_HEADS * HEAD_SIZE).astype(jnp.bfloat16), log_total)


def attend_back(query_rows, keys, values, mask, log_total, mixture, mixture_gradient):
    row_entries = query_rows.shape[0]
    head_group = QUERY_HEADS // KEY_VALUE_HEADS
    scale = 1.0 / math.sqrt(HEAD_SIZE)
    grouped_queries = query_rows.reshape(
        row_entries, KEY_VALUE_HEADS, head_group, HEAD_SIZE
    ).transpose(1, 0, 2, 3)
    gradient_groups = mixture_gradient.reshape(
        row_entries, KEY_VALUE_HEADS, head_group, HEAD_SIZE
    ).transpose(1, 0, 2, 3)
    mixture_groups = mixture.reshape(row_entries, KEY_VALUE_HEADS, head_group, HEAD_SIZE).transpose(
        1, 0, 2, 3
    )
    key_groups = keys.transpose(1, 0, 2)
    value_groups = values.transpose(1, 0, 2)

    def one_group(item):
        query_one, key_one, value_one, total_one, mixed_one, grad_one = item
        scores = (
            jnp.einsum("tgd,sd->gts", query_one, key_one, preferred_element_type=jnp.float32)
            * scale
        )
        scores = jnp.where(mask[None], scores, masked_score)
        probs = jnp.exp(scores - total_one)
        delta = jnp.einsum("tgd,tgd->gt", grad_one, mixed_one, preferred_element_type=jnp.float32)
        grad_probs = jnp.einsum(
            "tgd,sd->gts", grad_one, value_one, preferred_element_type=jnp.float32
        )
        grad_scores = (probs * (grad_probs - delta[..., None]) * scale).astype(jnp.bfloat16)
        grad_query = jnp.einsum(
            "gts,sd->tgd", grad_scores, key_one, preferred_element_type=jnp.float32
        )
        key_gradient = jnp.einsum(
            "gts,tgd->sd", grad_scores, query_one, preferred_element_type=jnp.float32
        )
        value_gradient = jnp.einsum(
            "gts,tgd->sd", probs.astype(jnp.bfloat16), grad_one, preferred_element_type=jnp.float32
        )
        return (grad_query, key_gradient, value_gradient)

    grad_query, key_gradient, value_gradient = lax.map(
        one_group,
        (grouped_queries, key_groups, value_groups, log_total, mixture_groups, gradient_groups),
    )
    grad_query = grad_query.transpose(1, 0, 2, 3).reshape(row_entries, QUERY_HEADS, HEAD_SIZE)
    return (grad_query, key_gradient.transpose(1, 0, 2), value_gradient.transpose(1, 0, 2))


def adam_update(params, first, second, grads):
    first_new = beta_one * first + (1.0 - beta_one) * grads
    second_new = beta_two * second + (1.0 - beta_two) * grads * grads
    corr_one = 1.0 - beta_one**ADAM_STEP
    corr_two = 1.0 - beta_two**ADAM_STEP
    moved = first_new / corr_one / (jnp.sqrt(second_new / corr_two) + adam_eps)
    return (params - learn_rate * (moved + decay_rate * params), first_new, second_new)


def owner_layout(term, owners, pair):
    columns = term.shape[0] // owners
    padded_columns = columns + -columns % pair
    table = term.reshape(owners, columns)
    return (jnp.pad(table, ((0, 0), (0, padded_columns - columns))).reshape(-1), columns)


def body(
    tokens,
    cotangent,
    seq_lengths,
    attn_params,
    attn_first,
    attn_second,
    ffn_params,
    ffn_first,
    ffn_second,
):
    row_entries = tokens.shape[0]
    ctx_count = lax.axis_size("ctx")
    ctx_index = lax.axis_index("ctx")
    owners = lax.axis_size("shard")
    slot_entries = row_entries * ctx_count
    length = seq_lengths[0]
    low_params = (attn_params.astype(jnp.bfloat16), ffn_params.astype(jnp.bfloat16))
    attn_whole, ffn_whole = (
        lax.all_gather(low_params[0], "shard", axis=0, tiled=True),
        lax.all_gather(low_params[1], "shard", axis=0, tiled=True),
    )
    w_query, key_matrix, value_matrix, w_out, gain_one, gain_two = split_attention(attn_whole)
    w_gate, w_up, w_down = split_feedforward(ffn_whole)
    gain_one = gain_one.astype(jnp.float32)
    gain_two = gain_two.astype(jnp.float32)
    positions = ctx_index * row_entries + jnp.arange(row_entries)
    key_positions = jnp.arange(slot_entries)
    valid = (positions < length).astype(jnp.float32)[:, None]
    has_rows = ctx_index * row_entries < length
    mask = (key_positions[None, :] <= positions[:, None]) & (key_positions[None, :] < length)
    inputs = tokens.astype(jnp.float32)
    scaled_one, inv_one, first_normed = norm_rows(inputs, gain_one)
    query_raw = jnp.dot(first_normed, w_query, preferred_element_type=jnp.float32).reshape(
        row_entries, QUERY_HEADS, HEAD_SIZE
    )
    unrotated_key = jnp.dot(first_normed, key_matrix, preferred_element_type=jnp.float32).reshape(
        row_entries, KEY_VALUE_HEADS, HEAD_SIZE
    )
    value_reduced = jnp.dot(first_normed, value_matrix, preferred_element_type=jnp.float32).astype(
        jnp.bfloat16
    )
    cosine_table, sine_table = rope_tables(positions)
    query_low = apply_rotation(query_raw, cosine_table, sine_table).astype(jnp.bfloat16)
    key_reduced = (
        apply_rotation(unrotated_key, cosine_table, sine_table)
        .astype(jnp.bfloat16)
        .reshape(row_entries, KEY_VALUE_HEADS * HEAD_SIZE)
    )
    full_keys, full_values = (
        lax.all_gather(key_reduced, "ctx", axis=0, tiled=True),
        lax.all_gather(value_reduced, "ctx", axis=0, tiled=True),
    )
    full_keys = full_keys.reshape(slot_entries, KEY_VALUE_HEADS, HEAD_SIZE)
    full_values = full_values.reshape(slot_entries, KEY_VALUE_HEADS, HEAD_SIZE)
    mixture, log_total = lax.cond(
        has_rows,
        lambda: attend(query_low, full_keys, full_values, mask),
        lambda: (
            jnp.zeros((row_entries, QUERY_HEADS * HEAD_SIZE), jnp.bfloat16),
            jnp.zeros(
                (KEY_VALUE_HEADS, QUERY_HEADS // KEY_VALUE_HEADS, row_entries, 1), jnp.float32
            ),
        ),
    )
    hidden = inputs + jnp.dot(mixture, w_out, preferred_element_type=jnp.float32)
    scaled_two, inv_two, normed_two = norm_rows(hidden, gain_two)
    gate = jnp.dot(normed_two, w_gate, preferred_element_type=jnp.float32)
    upward = jnp.dot(normed_two, w_up, preferred_element_type=jnp.float32)
    sigma = jax.nn.sigmoid(gate)
    activ = (gate * sigma * upward).astype(jnp.bfloat16)
    result = hidden + jnp.dot(activ, w_down, preferred_element_type=jnp.float32)
    outputs = (valid * result).astype(jnp.bfloat16)
    grad_result = valid * cotangent.astype(jnp.float32)
    grad_low = grad_result.astype(jnp.bfloat16)
    grad_w_down = jnp.dot(activ.T, grad_low, preferred_element_type=jnp.float32)
    grad_activ = jnp.dot(grad_low, w_down.T, preferred_element_type=jnp.float32)
    grad_gate = (grad_activ * upward * sigma * (1.0 + gate * (1.0 - sigma))).astype(jnp.bfloat16)
    grad_upward = (grad_activ * gate * sigma).astype(jnp.bfloat16)
    grad_w_gate = jnp.dot(normed_two.T, grad_gate, preferred_element_type=jnp.float32)
    grad_w_up = jnp.dot(normed_two.T, grad_upward, preferred_element_type=jnp.float32)
    ffn_term = jnp.concatenate(
        [grad_w_gate.reshape(-1), grad_w_up.reshape(-1), grad_w_down.reshape(-1)]
    )
    ffn_padded, ffn_columns = owner_layout(ffn_term, owners, ctx_count)
    grad_normed_two = jnp.dot(grad_gate, w_gate.T, preferred_element_type=jnp.float32) + jnp.dot(
        grad_upward, w_up.T, preferred_element_type=jnp.float32
    )
    grad_hidden_part, grad_gain_two = norm_back(grad_normed_two, scaled_two, inv_two, gain_two)
    grad_hidden = grad_result + grad_hidden_part
    grad_hidden_low = grad_hidden.astype(jnp.bfloat16)
    grad_w_out = jnp.dot(mixture.T, grad_hidden_low, preferred_element_type=jnp.float32)
    mixture_gradient = jnp.dot(grad_hidden_low, w_out.T, preferred_element_type=jnp.float32).astype(
        jnp.bfloat16
    )
    grad_query, full_key_gradient, full_value_gradient = lax.cond(
        has_rows,
        lambda: attend_back(
            query_low, full_keys, full_values, mask, log_total, mixture, mixture_gradient
        ),
        lambda: (
            jnp.zeros((row_entries, QUERY_HEADS, HEAD_SIZE), jnp.float32),
            jnp.zeros((slot_entries, KEY_VALUE_HEADS, HEAD_SIZE), jnp.float32),
            jnp.zeros((slot_entries, KEY_VALUE_HEADS, HEAD_SIZE), jnp.float32),
        ),
    )
    key_gradient, value_gradient = (
        lax.psum_scatter(
            full_key_gradient.reshape(slot_entries, KEY_VALUE_HEADS * HEAD_SIZE),
            "ctx",
            scatter_dimension=0,
            tiled=True,
        ),
        lax.psum_scatter(
            full_value_gradient.reshape(slot_entries, KEY_VALUE_HEADS * HEAD_SIZE),
            "ctx",
            scatter_dimension=0,
            tiled=True,
        ),
    )
    grad_query_raw = (
        reverse_rotation(grad_query, cosine_table, sine_table)
        .astype(jnp.bfloat16)
        .reshape(row_entries, QUERY_HEADS * HEAD_SIZE)
    )
    unrotated_key_gradient = (
        reverse_rotation(
            key_gradient.reshape(row_entries, KEY_VALUE_HEADS, HEAD_SIZE), cosine_table, sine_table
        )
        .astype(jnp.bfloat16)
        .reshape(row_entries, KEY_VALUE_HEADS * HEAD_SIZE)
    )
    plain_value_gradient = value_gradient.astype(jnp.bfloat16)
    grad_w_query = jnp.dot(first_normed.T, grad_query_raw, preferred_element_type=jnp.float32)
    grad_w_key = jnp.dot(first_normed.T, unrotated_key_gradient, preferred_element_type=jnp.float32)
    grad_w_value = jnp.dot(first_normed.T, plain_value_gradient, preferred_element_type=jnp.float32)
    grad_normed_one = jnp.dot(grad_query_raw, w_query.T, preferred_element_type=jnp.float32)
    grad_normed_one = grad_normed_one + jnp.dot(
        unrotated_key_gradient, key_matrix.T, preferred_element_type=jnp.float32
    )
    grad_normed_one = grad_normed_one + jnp.dot(
        plain_value_gradient, value_matrix.T, preferred_element_type=jnp.float32
    )
    grad_input_part, grad_gain_one = norm_back(grad_normed_one, scaled_one, inv_one, gain_one)
    grad_tokens = (grad_hidden + grad_input_part).astype(jnp.bfloat16)
    attn_term = jnp.concatenate(
        [
            grad_w_query.reshape(-1),
            grad_w_key.reshape(-1),
            grad_w_value.reshape(-1),
            grad_w_out.reshape(-1),
            grad_gain_one,
            grad_gain_two,
        ]
    )
    attn_padded, attn_columns = owner_layout(attn_term, owners, ctx_count)
    attn_half, ffn_half = (
        lax.psum_scatter(attn_padded, ("shard", "ctx"), scatter_dimension=0, tiled=True),
        lax.psum_scatter(ffn_padded, ("shard", "ctx"), scatter_dimension=0, tiled=True),
    )
    attn_joined, ffn_joined = (
        lax.all_gather(attn_half, "ctx", axis=0, tiled=True),
        lax.all_gather(ffn_half, "ctx", axis=0, tiled=True),
    )
    attn_grad = attn_joined[:attn_columns]
    attn_new, attn_first_new, attn_second_new = adam_update(
        attn_params, attn_first, attn_second, attn_grad
    )
    ffn_new, ffn_first_new, ffn_second_new = adam_update(
        ffn_params, ffn_first, ffn_second, ffn_joined
    )
    return (
        outputs,
        grad_tokens,
        attn_grad,
        ffn_joined,
        attn_new,
        attn_first_new,
        attn_second_new,
        ffn_new,
        ffn_first_new,
        ffn_second_new,
    )


def solution(mesh):
    return jax.shard_map(
        body,
        mesh=mesh,
        in_specs=(
            P(("shard", "ctx"), None),
            P(("shard", "ctx"), None),
            P("shard"),
            P("shard"),
            P("shard"),
            P("shard"),
            P("shard"),
            P("shard"),
            P("shard"),
        ),
        out_specs=(
            P(("shard", "ctx"), None),
            P(("shard", "ctx"), None),
            P("shard"),
            P("shard"),
            P("shard"),
            P("shard"),
            P("shard"),
            P("shard"),
            P("shard"),
            P("shard"),
        ),
        check_vma=False,
    )
```

profile of v0, /device:TPU:0, one launch (start us, length us, event | category | flops | bytes accessed | tf_op | source)
XLA Modules:
  0.0 597.9 jit_solution(964759938562371816)
XLA Ops:
  16.1 95.9 %all-reduce.9.cloned.1.call-done = bf16[885888]{0:T(1024)(128)(2,1)} async-done(((bf16[885888]{0:T(1024)(128)(2,1)}), bf16[885888]{0:T(1024)(128)(2,1)}) %all-reduce.9.cloned.1.call-update) | async-done | bytes 1771792
  112.0 1.4 fusion.89
  119.5 5.3 all_gather.19
  125.2 5.3 all_gather.20
  131.9 4.6 conditional.2
  134.5 2.0 fusion.3
  137.3 33.6 %all-gather.2.cloned.1.call-done = bf16[2654208]{0:T(1024)(128)(2,1)} async-done(((bf16[165888]{0:T(1024)(128)(2,1)}), bf16[2654208]{0:T(1024)(128)(2,1)}) %all-gather.2.cloned.1.call-update) | async-done | bytes 5308432 | tf_op jit(solution)/shard_map/all_gather | solution.py:191
  170.9 4.7 fusion.88
  175.6 3.0 slice.124
  178.6 3.6 slice.126
  182.1 3.4 fusion.93
  185.6 2.0 fusion.94
  187.5 4.3 slice.128
  191.9 4.8 multiply_convert_fusion
  200.2 1.6 fusion.69
  201.8 27.9 %conditional.3 = (f32[256,9,64]{0,2,1:T(8,128)}, f32[512,3,64]{0,2,1:T(8,128)}, f32[512,3,64]{0,2,1:T(8,128)}) conditional(s32[]{:T(128)} %convert_element_type.112, () %tuple.30, (bf16[256,9,64]{0,2,1:T(8,128)(2,1)S(1)}, bf16[512,3,64]{0,2,1:T(8,128)(2,1)}, bf16[512,3,64]{0,2,1:T(8,128)(2,1)}, bf16[256,576]{0,1:T(8,128)(2,1)S(1)}, ...), branch_computations={%region_7.8_spmd, %region_8.0_spmd} | conditional | flops 254999808 | bytes 16739761 | solution.py:266
  201.8 27.9 %while.13 = (s32[]{:T(128)}, f32[3,256,3,64]{1,3,2,0:T(8,128)}, f32[3,512,64]{1,2,0:T(8,128)}, f32[3,512,64]{1,2,0:T(8,128)}, bf16[3,512,64]{1,2,0:T(8,128)(2,1)...) while((s32[]{:T(128)}, f32[3,256,3,64]{1,3,2,0:T(8,128)}, ...), condition=%wide.region_10.10_spmd, body=%wide.region_9.9_spmd.sunk | while | flops 254999808 | bytes 16739633 | solution.py:147
  202.5 1.5 fusion.157
  205.8 1.4 fusion.158
  207.2 1.8 fusion.159
  211.8 1.5 fusion.157
  215.1 1.4 fusion.158
  216.5 1.8 fusion.159
  221.1 1.5 fusion.157
  224.4 1.4 fusion.158
  225.8 1.8 fusion.159
  231.2 2.7 fusion.61
  236.2 1.7 reshape.293
  238.0 1.9 reshape.296
  239.9 5.4 reshape.299
  245.3 2.4 fusion.97
  247.6 4.6 reshape.298
  252.3 2.4 fusion.96
  254.7 4.6 reshape.297
  259.3 11.2 %pad_maximum_fusion = f32[2654208]{0:T(1024)} fusion(f32[884736]{0:T(1024)} %reshape.299, f32[884736]{0:T(1024)} %reshape.298, f32[884736]{0:T(1024)} %reshape.297), kind=kLoop, calls=%fused_computation.50 | loop fusion | flops 5308416 | bytes 21233664 | tf_op jit(solution)/shard_map/concatenate | solution.py:252
  274.4 2.1 reshape.294
  278.9 2.0 fusion.74
  280.9 2.3 reshape.295
  283.2 2.9 fusion.50
  286.1 25.4 %concatenate.37 = f32[885888]{0:T(1024)} concatenate(f32[331776]{0:T(1024)S(1)} %copy-done.16, f32[110592]{0:T(1024)} %reshape.294, f32[110592]{0:T(1024)} %reshape.295, f32[331776]{0:T(1024)S(1)} %reshape.296, f32[576]{0:T(1024)S(1)} %get-tuple-element.157, f32[576]{0:T(1024)S(1)} %copy-done.48), dimensions={0} | concatenate | bytes 7087104 | tf_op jit(solution)/shard_map/concatenate | solution.py:316
  313.4 2.8 fusion.38
  317.2 242.8 %all-reduce.13.cloned.1.call-done = (f32[885888]{0:T(1024)}, f32[2654208]{0:T(1024)}) async-done(((f32[885888]{0:T(1024)}, f32[2654208]{0:T(1024)}), (f32[885888]{0:T(1024)}, f32[2654208]{0:T(1024)})) %all-reduce.13.cloned.1.call-update) | async-done | bytes 14160400
  560.1 1.4 dynamic-slice_dynamic-update-slice_fusion
  563.3 12.8 %all_gather.23 = f32[165888]{0:T(1024)S(1)} all-gather(f32[82944]{0:T(1024)S(1)} %dynamic-slice.3), channel_id=1, replica_groups=mesh['shard'=16,'ctx'=2] {'ctx'}, dimensions={0}, use_global_device_ids=true | all-gather | bytes 995328 | tf_op jit(solution)/shard_map/all_gather | solution.py:333
  576.1 1.6 multiply_subtract_fusion
  577.7 8.9 %all-reduce.11.cloned.1.call-done = f32[55368]{0:T(1024)} async-done(((f32[55368]{0:T(1024)}), f32[55368]{0:T(1024)}) %all-reduce.11.cloned.1.call-update) | async-done | bytes 221488
  586.6 1.9 multiply_subtract_fusion.1
  588.5 1.6 copy.105
  (234 shorter events, 50.2 us)
Async XLA Ops:
  7.2 104.9 %all-reduce.9.cloned.1.call-start = ((), (), s32[]{:S(2)}) async-start(), calls=%async_computation.5 | async-start | bytes 3547136
  10.1 2.7 copy-start.26
  10.2 4.1 copy-start
  12.7 158.1 %all-gather.2.cloned.1.call-start = ((), (), s32[]{:S(2)}) async-start(), calls=%async_computation.2 | async-start | bytes 5640192 | tf_op jit(solution)/shard_map/all_gather | solution.py:191
  13.6 257.0 %reduce-scatter.3.cloned.1.call-start = ((), (), s32[]{:S(2)}) async-start(), calls=%async_computation.3 | async-start | bytes 589824 | tf_op jit(solution)/shard_map/reduce_scatter | solution.py:278
  14.7 116.4 %copy-start.32 = (f32[256,64]{0,1:T(8,128)}, f32[256,64]{0,1:T(8,128)S(1)}, u32[]{:S(2)}) copy-start(f32[256,64]{0,1:T(8,128)S(1)} %get-tuple-element.211) | copy-start | bytes 196612
  14.7 116.4 %copy-start.34 = (f32[256,64]{0,1:T(8,128)}, f32[256,64]{0,1:T(8,128)S(1)}, u32[]{:S(2)}) copy-start(f32[256,64]{0,1:T(8,128)S(1)} %get-tuple-element.212) | copy-start | bytes 196612
  114.0 2.7 copy-start.12
  115.7 3.8 copy-start.28
  116.7 8.1 %copy-start.38 = (bf16[576,192]{1,0:T(8,128)(2,1)}, bf16[576,192]{1,0:T(8,128)(2,1)S(1)}, u32[]{:S(2)}) copy-start(bf16[576,192]{1,0:T(8,128)(2,1)S(1)} %reshape.286) | copy-start | bytes 663556
  117.3 19.3 %copy-start.10 = (bf16[576,576]{1,0:T(8,128)(2,1)}, bf16[576,576]{1,0:T(8,128)(2,1)S(1)}, u32[]{:S(2)}) copy-start(bf16[576,576]{1,0:T(8,128)(2,1)S(1)} %reshape.288) | copy-start | bytes 1990660
  124.8 7.1 %copy-start.30 = (bf16[512,192]{0,1:T(8,128)(2,1)}, bf16[512,192]{0,1:T(8,128)(2,1)S(1)}, u32[]{:S(2)}) copy-start(bf16[512,192]{0,1:T(8,128)(2,1)S(1)} %all_gather.19) | copy-start | bytes 589828
  137.2 48.3 %copy-start.7 = (bf16[256,576]{0,1:T(8,128)(2,1)}, bf16[256,576]{0,1:T(8,128)(2,1)S(1)}, u32[]{:S(2)}) copy-start(bf16[256,576]{0,1:T(8,128)(2,1)S(1)} %multiply_convert_fusion.3) | copy-start | bytes 884740
  187.5 4.3 copy-start.39
  191.9 4.8 copy-start.1
  201.8 2.5 copy-start.17
  205.8 3.2 copy-start.18
  205.8 4.3 copy-start.3
  207.2 3.9 copy-start.15
  211.1 2.5 copy-start.17
  215.1 3.2 copy-start.18
  215.1 4.3 copy-start.3
  216.5 3.9 copy-start.15
  224.4 3.2 copy-start.18
  224.4 4.3 copy-start.3
  225.8 3.9 copy-start.15
  229.7 49.2 %reduce-scatter.5.cloned.1.call-start = ((), (), s32[]{:S(2)}) async-start(), calls=%async_computation.4 | async-start | bytes 589824 | tf_op jit(solution)/shard_map/reduce_scatter | solution.py:284
  231.2 2.7 copy-start.33
  239.9 5.4 copy-start.8
  239.9 5.4 copy-start.20
  247.6 4.7 copy-start.22
  259.3 11.3 %copy-start.35 = (f32[256,64]{0,1:T(8,128)S(1)}, f32[256,64]{0,1:T(8,128)}, u32[]{:S(2)}) copy-start(f32[256,64]{0,1:T(8,128)} %copy-done.34) | copy-start | bytes 196612
  259.3 300.8 %all-reduce.13.cloned.1.call-start = ((), (), s32[]{:S(2)}) async-start(), calls=%async_computation.7 | async-start | bytes 28327936
  271.5 5.0 copy-start.29
  271.6 6.1 %copy-start.13 = (bf16[576,576]{1,0:T(8,128)(2,1)S(1)}, bf16[576,576]{1,0:T(8,128)(2,1)}, u32[]{:S(2)}) copy-start(bf16[576,576]{1,0:T(8,128)(2,1)} %copy-done.12) | copy-start | bytes 1990660
  271.6 6.1 %copy-start.25 = (bf16[256,9,64]{0,2,1:T(8,128)(2,1)S(1)}, bf16[256,9,64]{0,2,1:T(8,128)(2,1)}, u32[]{:S(2)}) copy-start(bf16[256,9,64]{0,2,1:T(8,128)(2,1)} %copy-done.24) | copy-start | bytes 884740
  280.9 5.2 copy-start.16
  280.9 5.2 copy-start.48
  311.5 275.1 %all-reduce.11.cloned.1.call-start = ((), (), s32[]{:S(2)}) async-start(), calls=%async_computation.6 | async-start | bytes 450560
  313.4 2.9 copy-start.52
  313.4 2.9 copy-start.5
  313.4 2.9 copy-start.31
  316.3 259.8 %copy-start.27 = (f32[165888]{0:T(1024)S(1)}, f32[165888]{0:T(1024)}, u32[]{:S(2)}) copy-start(f32[165888]{0:T(1024)} %param.21) | copy-start | bytes 1990660
  316.3 259.8 %copy-start.44 = (f32[165888]{0:T(1024)S(1)}, f32[165888]{0:T(1024)}, u32[]{:S(2)}) copy-start(f32[165888]{0:T(1024)} %param.22) | copy-start | bytes 1990660
  316.3 259.7 %copy-start.45 = (f32[165888]{0:T(1024)S(1)}, f32[165888]{0:T(1024)}, u32[]{:S(2)}) copy-start(f32[165888]{0:T(1024)} %param.23) | copy-start | bytes 1990660
  576.1 10.6 %copy-start.41 = (f32[55368]{0:T(1024)S(1)}, f32[55368]{0:T(1024)}, u32[]{:S(2)}) copy-start(f32[55368]{0:T(1024)} %param.18) | copy-start | bytes 664420
  576.1 10.6 %copy-start.46 = (f32[55368]{0:T(1024)S(1)}, f32[55368]{0:T(1024)}, u32[]{:S(2)}) copy-start(f32[55368]{0:T(1024)} %param.19) | copy-start | bytes 664420
  576.1 10.6 %copy-start.47 = (f32[55368]{0:T(1024)S(1)}, f32[55368]{0:T(1024)}, u32[]{:S(2)}) copy-start(f32[55368]{0:T(1024)} %param.20) | copy-start | bytes 664420
  (24 other events, 38.9 us)
Sparse Core Ops, SparseCore 0:
  12.9 99.1 all-reduce.8
  114.8 56.0 all-gather.1
  229.8 11.7 reduce-scatter.2
  259.4 11.7 reduce-scatter.4
  311.7 248.3 all-reduce.12
  562.8 23.7 all-reduce.10
where the time goes:
time: 600 us; the launch traced here: 598 us
  waiting for transfers between devices  381 us (64%)
  local copies, waits for them, and re-layouts  88.9 us (15%)
  matrix products  58.9 us (10%)
  other arithmetic  27.6 us (5%)
  blocking collectives  23.4 us (4%)
  between operations  16.8 us (3%)
    unnamed x9, waiting for transfers between devices  348 us
    all_gather x1, waiting for transfers between devices, body(): lax.all_gather(low_params[1], 'shard', axis=0, tiled=True)  33.6 us
    concatenate x1, local copies, waits for them, and re-layouts, body(): jnp.concatenate([grad_w_query.reshape(-1), grad_w_key.reshape(-1), grad_w...  25.4 us
    slice x6, local copies, waits for them, and re-layouts, split_flattened(): pieces.append(flattened[offset:offset + width].reshape(shape))  18 us
    unnamed x105, local copies, waits for them, and re-layouts  13.8 us
    all_gather x1, blocking collectives, body(): lax.all_gather(ffn_half, 'ctx', axis=0, tiled=True)  12.8 us
  transfers between devices with their start and end apart: 6, of which 4 were waited for; matrix products, arithmetic and copies ran while one was open for 12% of the time, Pallas kernels for 0%

commit v1 on v0

--- a/solution.py
+++ b/solution.py
@@ -3,6 +3,7 @@
 import jax.numpy as jnp
 from jax import lax
 from jax.sharding import PartitionSpec as P
+from jax.lax import axis_index, axis_size, ppermute
 
 MODEL_WIDTH = 576
 QUERY_HEADS = 9
@@ -18,6 +19,12 @@
 decay_rate = 0.1
 adam_eps = 1e-08
 masked_score = -1e30
+
+
+def edges_play(raw, dim_k):
+    carry_out = list(raw.shape[1:])
+    carry_out[dim_k] *= raw.shape[0]
+    return jnp.moveaxis(raw, 0, dim_k).reshape(carry_out)
 
 
 def split_flattened(flattened, shapes):
@@ -186,9 +193,31 @@
     slot_entries = row_entries * ctx_count
     length = seq_lengths[0]
     low_params = (attn_params.astype(jnp.bfloat16), ffn_params.astype(jnp.bfloat16))
+
+    def obtain_strings(row_data, shard_axis, array_dim):
+        amount_of = axis_size(shard_axis)
+        pages = tuple(((dev, (dev + 1) % amount_of) for dev in range(amount_of)))
+        local_next, carry_in = ([], [])
+        buffers = tuple(((dev_i, i) for i, dev_i in pages))
+        for k in range(amount_of - 1):
+            if k % 2 == 0:
+                piece_now = ppermute(
+                    local_next[-1] if local_next else row_data, axis_name=shard_axis, perm=pages
+                )
+                local_next.append(piece_now)
+            else:
+                built = ppermute(carry_in[-1] if carry_in else row_data, shard_axis, perm=buffers)
+                carry_in.append(built)
+        local_out = jnp.stack([*local_next[::-1], row_data, *carry_in], axis=0)
+        tall = axis_index(shard_axis)
+        inter = len(local_next)
+        part_now = tall - inter
+        local_out = local_out[(jnp.arange(amount_of) - part_now) % amount_of]
+        return edges_play(local_out, array_dim)
+
     attn_whole, ffn_whole = (
         lax.all_gather(low_params[0], "shard", axis=0, tiled=True),
-        lax.all_gather(low_params[1], "shard", axis=0, tiled=True),
+        obtain_strings(low_params[1], "shard", 0),
     )
     w_query, key_matrix, value_matrix, w_out, gain_one, gain_two = split_attention(attn_whole)
     w_gate, w_up, w_down = split_feedforward(ffn_whole)

time: 600 us -> 689 us (1.15); the launches traced: 598 us -> 675 us
  local copies, waits for them, and re-layouts: 88.9 us -> 171 us
  waiting for transfers between devices: 381 us -> 345 us
  starting transfers between devices: 0.47 us -> 30.6 us
    another operation x0 -> x17, local copies, waits for them, and re-layouts: none -> 56.1 us  [obtain_strings(): local_out = jnp.stack([*local_next[::-1], row_data, *carry_in], axis=0)]
    all_gather x1 -> x0, waiting for transfers between devices: 33.6 us -> none  [body(): lax.all_gather(low_params[1], 'shard', axis=0, tiled=True)]
    ppermute x0 -> x15, starting transfers between devices: none -> 30.4 us  [the longest x7 29.3 us: obtain_strings(): ppermute(carry_in[-1] if carry_in else row_data, shard_axis, perm=buffers)]
    unnamed x9 -> x8, waiting for transfers between devices: 348 us -> 329 us
    gather x0 -> x3, local copies, waits for them, and re-layouts: none -> 16.7 us  [obtain_strings(): local_out = local_out[(jnp.arange(amount_of) - part_now) % amount_of]]
    ppermute x0 -> x15, waiting for transfers between devices: none -> 16.6 us  [the longest x8 14.6 us: obtain_strings(): ppermute(local_next[-1] if local_next else row_data, axis_name=shard_axis...]
    slice x6 -> x4, local copies, waits for them, and re-layouts: 18 us -> 24.7 us  [split_flattened(): pieces.append(flattened[offset:offset + width].reshape(shape))]
  transfers between devices with their start and end apart: 6 -> 20, of which waited for: 4 -> 9; matrix products, arithmetic and copies ran while one was open for 12% -> 15% of each run, Pallas kernels for 0% -> 0%
where the time goes in v1:
time: 689 us; the launch traced here: 675 us
  waiting for transfers between devices  345 us (50%)
  local copies, waits for them, and re-layouts  171 us (25%)
  matrix products  56.2 us (8%)
  other arithmetic  30.7 us (4%)
  starting transfers between devices  30.6 us (4%)
  blocking collectives  24.7 us (4%)
  between operations  16.7 us (2%)
    unnamed x8, waiting for transfers between devices  329 us
    another operation x17, local copies, waits for them, and re-layouts, obtain_strings(): local_out = jnp.stack([*local_next[::-1], row_data, *carry_in], axis=0)  56.1 us
    ppermute x7, starting transfers between devices, obtain_strings(): ppermute(carry_in[-1] if carry_in else row_data, shard_axis, perm=buffers)  29.3 us
    concatenate x1, local copies, waits for them, and re-layouts, body(): jnp.concatenate([grad_w_query.reshape(-1), grad_w_key.reshape(-1), grad_w...  27.3 us
    slice x4, local copies, waits for them, and re-layouts, split_flattened(): pieces.append(flattened[offset:offset + width].reshape(shape))  24.7 us
    unnamed x105, local copies, waits for them, and re-layouts  18.5 us
    gather x3, local copies, waits for them, and re-layouts, obtain_strings(): local_out = local_out[(jnp.arange(amount_of) - part_now) % amount_of]  16.7 us
    ppermute x8, waiting for transfers between devices, obtain_strings(): ppermute(local_next[-1] if local_next else row_data, axis_name=shard_axis...  14.6 us
  transfers between devices with their start and end apart: 20, of which 9 were waited for; matrix products, arithmetic and copies ran while one was open for 15% of the time, Pallas kernels for 0%

profile of v1, /device:TPU:0, one launch (start us, length us, event | category | flops | bytes accessed | tf_op | source)
XLA Modules:
  0.0 675.2 jit_solution(13604373827844746288)
XLA Ops:
  8.9 5.0 collective-permute-start.8
  21.6 4.4 collective-permute-start.9
  26.8 2.0 stack.58
  30.0 4.7 collective-permute-done.1
  34.7 2.0 stack.57
  38.7 4.5 collective-permute-start.10
  43.2 75.8 %all-reduce.9.cloned.1.call-done = bf16[885888]{0:T(1024)(128)(2,1)} async-done(((bf16[885888]{0:T(1024)(128)(2,1)}), bf16[885888]{0:T(1024)(128)(2,1)}) %all-reduce.9.cloned.1.call-update) | async-done | bytes 1771792
  128.5 4.5 collective-permute-start.11
  133.0 3.3 collective-permute-done.3
  137.9 4.6 collective-permute-start.12
  142.5 3.3 collective-permute-done.4
  147.2 4.8 collective-permute-start.13
  152.0 3.3 collective-permute-done.5
  155.2 6.3 all_gather.16
  162.2 5.4 all_gather.17
  167.6 5.8 conditional.2
  171.2 2.2 fusion.3
  178.7 2.0 stack.62
  180.7 2.0 stack.55
  184.9 2.0 stack.64
  187.0 2.1 stack.53
  189.1 2.0 stack.65
  195.3 30.0 %stack.67 = bf16[16,165888]{1,0:T(8,128)(2,1)} concatenate(bf16[1,165888]{1,0:T(2,128)(2,1)} %stack.51, bf16[1,165888]{1,0:T(2,128)(2,1)} %stack.52, bf16[1,165888]{1,0:T(2,128)(2,1)} %stack.53, bf16[1,165888]{1,0:T(2,128)(2,1)} %stack.54, bf16[1,165888]{1,0:T(2,128)(2,1)} %stack.55, bf16[1,165888]{1,0:T(2,128)(2,1)} %stack.56, bf16[1,165888]{1,0:T(2,128)(2,1)} %stack.57, ...), dimensions={0} | concatenate | bytes 10616832 | tf_op jit(solution)/shard_map/stack | solution.py:211
  225.3 4.4 fusion.111
  229.8 8.2 %gather_fusion = bf16[16,82944]{1,0:T(8,128)(2,1)} fusion(bf16[16,82944]{1,0:T(8,128)(2,1)} %get-tuple-element.192, s32[1024]{0:T(1024)} %pad_clamp_fusion), kind=kCustom, calls=%fused_computation | custom fusion | bytes 5308480 | tf_op jit(solution)/shard_map/gather | solution.py:215
  238.0 3.5 constant_dynamic-update-slice_fusion.1
  241.5 4.0 gather_fusion.1
  245.5 3.4 constant_dynamic-update-slice_fusion
  248.9 10.2 %slice.103 = bf16[4608,576]{1,0:T(8,128)(2,1)} reshape(bf16[16,165888]{1,0:T(8,128)(2,1)} %constant_dynamic-update-slice_fusion) | data formatting | bytes 10616832 | tf_op jit(solution)/shard_map/slice | solution.py:37
  259.2 11.3 %slice.100 = bf16[1728,1536]{1,0:T(8,128)(2,1)} reshape(bf16[16,165888]{1,0:T(8,128)(2,1)} %constant_dynamic-update-slice_fusion) | data formatting | bytes 10616832 | tf_op jit(solution)/shard_map/slice | solution.py:37
  270.5 2.4 fusion.43
  272.9 2.4 fusion.37
  275.3 2.4 multiply_convert_fusion.1
  282.7 27.5 %conditional.3 = (f32[256,9,64]{0,2,1:T(8,128)}, f32[512,3,64]{0,2,1:T(8,128)}, f32[512,3,64]{0,2,1:T(8,128)}) conditional(s32[]{:T(128)} %convert_element_type.112, () %tuple.30, (bf16[256,9,64]{0,2,1:T(8,128)(2,1)}, bf16[512,3,64]{0,2,1:T(8,128)(2,1)}, bf16[512,3,64]{0,2,1:T(8,128)(2,1)}, bf16[256,576]{0,1:T(8,128)(2,1)S(1)}, ...), branch_computations={%region_7.8_spmd, %region_8.11_spmd} | conditional | flops 254999808 | bytes 9661705 | solution.py:295
  282.7 27.3 %while.13 = (s32[]{:T(128)}, f32[3,256,3,64]{1,3,2,0:T(8,128)}, f32[3,512,64]{1,2,0:T(8,128)}, f32[3,512,64]{1,2,0:T(8,128)}, bf16[3,512,64]{1,2,0:T(8,128)(2,1)...) while((s32[]{:T(128)}, f32[3,256,3,64]{1,3,2,0:T(8,128)}, ...), condition=%wide.region_10.10_spmd, body=%wide.region_9.9_spmd.sunk | while | flops 254999808 | bytes 9661577 | solution.py:154
  311.6 2.7 fusion.83
  319.3 5.3 reshape.331
  324.7 2.4 fusion.117
  327.1 4.7 reshape.330
  331.7 2.4 fusion.116
  334.1 4.5 reshape.329
  338.8 11.2 %pad_maximum_fusion = f32[2654208]{0:T(1024)} fusion(f32[884736]{0:T(1024)} %reshape.331, f32[884736]{0:T(1024)} %reshape.330, f32[884736]{0:T(1024)} %reshape.329), kind=kLoop, calls=%fused_computation.52 | loop fusion | flops 5308416 | bytes 21233664 | tf_op jit(solution)/shard_map/concatenate | solution.py:281
  358.9 27.3 %concatenate.37 = f32[885888]{0:T(1024)} concatenate(f32[331776]{0:T(1024)S(1)} %copy-done.10, f32[110592]{0:T(1024)S(1)} %copy-done.23, f32[110592]{0:T(1024)} %reshape.327, f32[331776]{0:T(1024)} %reshape.328, f32[576]{0:T(1024)S(1)} %get-tuple-element.157, f32[576]{0:T(1024)S(1)} %copy-done.45), dimensions={0} | concatenate | bytes 7087104 | tf_op jit(solution)/shard_map/concatenate | solution.py:345
  388.1 3.1 fusion.58
  392.2 245.2 %all-reduce.13.cloned.1.call-done = (f32[885888]{0:T(1024)}, f32[2654208]{0:T(1024)}) async-done(((f32[885888]{0:T(1024)}, f32[2654208]{0:T(1024)}), (f32[885888]{0:T(1024)}, f32[2654208]{0:T(1024)})) %all-reduce.13.cloned.1.call-update) | async-done | bytes 14160400
  640.6 12.9 %all_gather.19 = f32[165888]{0:T(1024)S(1)} all-gather(f32[82944]{0:T(1024)S(1)} %dynamic-slice.3), channel_id=1, replica_groups=mesh['shard'=16,'ctx'=2] {'ctx'}, dimensions={0}, use_global_device_ids=true | all-gather | bytes 995328 | tf_op jit(solution)/shard_map/all_gather | solution.py:362
  653.6 2.9 multiply_subtract_fusion
  656.4 7.6 %all-reduce.11.cloned.1.call-done = f32[55368]{0:T(1024)} async-done(((f32[55368]{0:T(1024)}), f32[55368]{0:T(1024)}) %all-reduce.11.cloned.1.call-update) | async-done | bytes 221488
  (245 shorter events, 97.3 us)
Async XLA Ops:
  7.2 111.7 %all-reduce.9.cloned.1.call-start = ((), (), s32[]{:S(2)}) async-start(), calls=%async_computation.4 | async-start | bytes 3547136
  8.3 13.2 %collective-permute-start = (bf16[165888]{0:T(1024)(128)(2,1)S(1)}, bf16[165888]{0:T(1024)(128)(2,1)}, u32[]{:S(2)}, u32[]{:S(2)}) collective-permute-start(bf16[165888]{0:T(1024)(128)(2,1)S(1)} %convert_element_type.123), channel_id=1, source_target_pairs={{0,2},{2,4},{4,6},{6,8},{8,10},{10,12},{12,14},{14,16},{16,18},{18... | collective-permute-start | bytes 995336 | tf_op jit(solution)/shard_map/ppermute | solution.py:204
  8.9 12.7 %collective-permute-start.8 = (bf16[165888]{0:T(1024)(128)(2,1)S(1)}, bf16[165888]{0:T(1024)(128)(2,1)S(1)}, u32[]{:S(2)}, u32[]{:S(2)}) collective-permute-start(bf16[165888]{0:T(1024)(128)(2,1)S(1)} %convert_element_type.123), channel_id=1, source_target_pairs={{2,0},{4,2},{6,4},{8,6},{10,8},{12,10},{14,12},{16,14},{18,16},{20... | collective-permute-start | bytes 995336 | tf_op jit(solution)/shard_map/ppermute | solution.py:209
  13.9 7.5 %copy-start = (bf16[256,576]{0,1:T(8,128)(2,1)S(1)}, bf16[256,576]{0,1:T(8,128)(2,1)}, u32[]{:S(2)}) copy-start(bf16[256,576]{0,1:T(8,128)(2,1)} %param.15) | copy-start | bytes 884740
  19.4 330.6 %reduce-scatter.3.cloned.1.call-start = ((), (), s32[]{:S(2)}) async-start(), calls=%async_computation.2 | async-start | bytes 589824 | tf_op jit(solution)/shard_map/reduce_scatter | solution.py:307
  20.7 125.1 %copy-start.24 = (f32[256,64]{0,1:T(8,128)}, f32[256,64]{0,1:T(8,128)S(1)}, u32[]{:S(2)}) copy-start(f32[256,64]{0,1:T(8,128)S(1)} %get-tuple-element.210) | copy-start | bytes 196612
  20.7 289.5 %copy-start.27 = (f32[256,64]{0,1:T(8,128)}, f32[256,64]{0,1:T(8,128)S(1)}, u32[]{:S(2)}) copy-start(f32[256,64]{0,1:T(8,128)S(1)} %get-tuple-element.211) | copy-start | bytes 196612
  21.5 13.2 %collective-permute-start.1 = (bf16[165888]{0:T(1024)(128)(2,1)}, bf16[165888]{0:T(1024)(128)(2,1)}, u32[]{:S(2)}, u32[]{:S(2)}) collective-permute-start(bf16[165888]{0:T(1024)(128)(2,1)} %collective-permute-done), channel_id=1, source_target_pairs={{0,2},{2,4},{4,6},{6,8},{8,10},{10,12},{12,14},{14,16},{16,18},{18... | collective-permute-start | bytes 995336 | tf_op jit(solution)/shard_map/ppermute | solution.py:204
  21.6 15.1 %collective-permute-start.9 = (bf16[165888]{0:T(1024)(128)(2,1)S(1)}, bf16[165888]{0:T(1024)(128)(2,1)}, u32[]{:S(2)}, u32[]{:S(2)}) collective-permute-start(bf16[165888]{0:T(1024)(128)(2,1)S(1)} %collective-permute-done.8), channel_id=1, source_target_pairs={{2,0},{4,2},{6,4},{8,6},{10,8},{12,10},{14,12},{16,14},{18,16},{20... | collective-permute-start | bytes 995336 | tf_op jit(solution)/shard_map/ppermute | solution.py:209
  34.7 91.8 %collective-permute-start.2 = (bf16[165888]{0:T(1024)(128)(2,1)}, bf16[165888]{0:T(1024)(128)(2,1)}, u32[]{:S(2)}, u32[]{:S(2)}) collective-permute-start(bf16[165888]{0:T(1024)(128)(2,1)} %collective-permute-done.1), channel_id=1, source_target_pairs={{0,2},{2,4},{4,6},{6,8},{8,10},{10,12},{12,14},{14,16},{16,18},{18... | collective-permute-start | bytes 995336 | tf_op jit(solution)/shard_map/ppermute | solution.py:204
  38.7 89.8 %collective-permute-start.10 = (bf16[165888]{0:T(1024)(128)(2,1)}, bf16[165888]{0:T(1024)(128)(2,1)}, u32[]{:S(2)}, u32[]{:S(2)}) collective-permute-start(bf16[165888]{0:T(1024)(128)(2,1)} %collective-permute-done.9), channel_id=1, source_target_pairs={{2,0},{4,2},{6,4},{8,6},{10,8},{12,10},{14,12},{16,14},{18,16},{20... | collective-permute-start | bytes 995336 | tf_op jit(solution)/shard_map/ppermute | solution.py:209
  126.5 9.7 %collective-permute-start.3 = (bf16[165888]{0:T(1024)(128)(2,1)}, bf16[165888]{0:T(1024)(128)(2,1)}, u32[]{:S(2)}, u32[]{:S(2)}) collective-permute-start(bf16[165888]{0:T(1024)(128)(2,1)} %collective-permute-done.2), channel_id=1, source_target_pairs={{0,2},{2,4},{4,6},{6,8},{8,10},{10,12},{12,14},{14,16},{16,18},{18... | collective-permute-start | bytes 995336 | tf_op jit(solution)/shard_map/ppermute | solution.py:204
  127.6 18.2 %copy-start.7 = (bf16[576,576]{1,0:T(8,128)(2,1)}, bf16[576,576]{1,0:T(8,128)(2,1)S(1)}, u32[]{:S(2)}) copy-start(bf16[576,576]{1,0:T(8,128)(2,1)S(1)} %reshape.314) | copy-start | bytes 1990660
  128.5 9.4 %collective-permute-start.11 = (bf16[165888]{0:T(1024)(128)(2,1)}, bf16[165888]{0:T(1024)(128)(2,1)S(1)}, u32[]{:S(2)}, u32[]{:S(2)}) collective-permute-start(bf16[165888]{0:T(1024)(128)(2,1)} %collective-permute-done.10), channel_id=1, source_target_pairs={{2,0},{4,2},{6,4},{8,6},{10,8},{12,10},{14,12},{16,14},{18,16},{20... | collective-permute-start | bytes 995336 | tf_op jit(solution)/shard_map/ppermute | solution.py:209
  136.2 9.6 %collective-permute-start.4 = (bf16[165888]{0:T(1024)(128)(2,1)}, bf16[165888]{0:T(1024)(128)(2,1)S(1)}, u32[]{:S(2)}, u32[]{:S(2)}) collective-permute-start(bf16[165888]{0:T(1024)(128)(2,1)} %collective-permute-done.3), channel_id=1, source_target_pairs={{0,2},{2,4},{4,6},{6,8},{8,10},{10,12},{12,14},{14,16},{16,18},{18... | collective-permute-start | bytes 995336 | tf_op jit(solution)/shard_map/ppermute | solution.py:204
  136.3 31.3 %copy-start.29 = (pred[256,512]{0,1:T(8,128)(4,1)S(1)}, pred[256,512]{0,1:T(8,128)(4,1)}, u32[]{:S(2)}) copy-start(pred[256,512]{0,1:T(8,128)(4,1)} %fusion.78) | copy-start | bytes 393220
  137.9 23.7 %copy-start.39 = (bf16[165888]{0:T(1024)(128)(2,1)}, bf16[165888]{0:T(1024)(128)(2,1)S(1)}, u32[]{:S(2)}) copy-start(bf16[165888]{0:T(1024)(128)(2,1)S(1)} %collective-permute-done.11) | copy-start | bytes 995332
  137.9 9.2 %collective-permute-start.12 = (bf16[165888]{0:T(1024)(128)(2,1)S(1)}, bf16[165888]{0:T(1024)(128)(2,1)}, u32[]{:S(2)}, u32[]{:S(2)}) collective-permute-start(bf16[165888]{0:T(1024)(128)(2,1)S(1)} %collective-permute-done.11), channel_id=1, source_target_pairs={{2,0},{4,2},{6,4},{8,6},{10,8},{12,10},{14,12},{16,14},{18,16},{20... | collective-permute-start | bytes 995336 | tf_op jit(solution)/shard_map/ppermute | solution.py:209
  145.8 15.8 %copy-start.41 = (bf16[165888]{0:T(1024)(128)(2,1)}, bf16[165888]{0:T(1024)(128)(2,1)S(1)}, u32[]{:S(2)}) copy-start(bf16[165888]{0:T(1024)(128)(2,1)S(1)} %collective-permute-done.4) | copy-start | bytes 995332
  145.8 9.4 %collective-permute-start.5 = (bf16[165888]{0:T(1024)(128)(2,1)S(1)}, bf16[165888]{0:T(1024)(128)(2,1)}, u32[]{:S(2)}, u32[]{:S(2)}) collective-permute-start(bf16[165888]{0:T(1024)(128)(2,1)S(1)} %collective-permute-done.4), channel_id=1, source_target_pairs={{0,2},{2,4},{4,6},{6,8},{8,10},{10,12},{12,14},{14,16},{16,18},{18... | collective-permute-start | bytes 995336 | tf_op jit(solution)/shard_map/ppermute | solution.py:204
  147.2 26.7 %collective-permute-start.13 = (bf16[165888]{0:T(1024)(128)(2,1)}, bf16[165888]{0:T(1024)(128)(2,1)}, u32[]{:S(2)}, u32[]{:S(2)}) collective-permute-start(bf16[165888]{0:T(1024)(128)(2,1)} %collective-permute-done.12), channel_id=1, source_target_pairs={{2,0},{4,2},{6,4},{8,6},{10,8},{12,10},{14,12},{16,14},{18,16},{20... | collective-permute-start | bytes 995336 | tf_op jit(solution)/shard_map/ppermute | solution.py:209
  155.2 20.2 %collective-permute-start.6 = (bf16[165888]{0:T(1024)(128)(2,1)}, bf16[165888]{0:T(1024)(128)(2,1)}, u32[]{:S(2)}, u32[]{:S(2)}) collective-permute-start(bf16[165888]{0:T(1024)(128)(2,1)} %collective-permute-done.5), channel_id=1, source_target_pairs={{0,2},{2,4},{4,6},{6,8},{8,10},{10,12},{12,14},{14,16},{16,18},{18... | collective-permute-start | bytes 995336 | tf_op jit(solution)/shard_map/ppermute | solution.py:204
  162.2 11.2 %copy-start.5 = (bf16[576,576]{1,0:T(8,128)(2,1)}, bf16[576,576]{1,0:T(8,128)(2,1)S(1)}, u32[]{:S(2)}) copy-start(bf16[576,576]{1,0:T(8,128)(2,1)S(1)} %reshape.320) | copy-start | bytes 1990660
  173.4 9.4 %copy-start.40 = (bf16[165888]{0:T(1024)(128)(2,1)S(1)}, bf16[165888]{0:T(1024)(128)(2,1)}, u32[]{:S(2)}) copy-start(bf16[165888]{0:T(1024)(128)(2,1)} %copy-done.39) | copy-start | bytes 995332
  173.8 11.1 %copy-start.11 = (f32[256,576]{0,1:T(8,128)}, f32[256,576]{0,1:T(8,128)S(1)}, u32[]{:S(2)}) copy-start(f32[256,576]{0,1:T(8,128)S(1)} %get-tuple-element.213) | copy-start | bytes 1769476
  173.8 10.0 %copy-start.42 = (bf16[165888]{0:T(1024)(128)(2,1)S(1)}, bf16[165888]{0:T(1024)(128)(2,1)}, u32[]{:S(2)}) copy-start(bf16[165888]{0:T(1024)(128)(2,1)} %copy-done.41) | copy-start | bytes 995332
  173.9 19.2 %collective-permute-start.14 = (bf16[165888]{0:T(1024)(128)(2,1)}, bf16[165888]{0:T(1024)(128)(2,1)S(1)}, u32[]{:S(2)}, u32[]{:S(2)}) collective-permute-start(bf16[165888]{0:T(1024)(128)(2,1)} %collective-permute-done.13), channel_id=1, source_target_pairs={{2,0},{4,2},{6,4},{8,6},{10,8},{12,10},{14,12},{16,14},{18,16},{20... | collective-permute-start | bytes 995336 | tf_op jit(solution)/shard_map/ppermute | solution.py:209
  175.4 18.8 %collective-permute-start.7 = (bf16[165888]{0:T(1024)(128)(2,1)}, bf16[165888]{0:T(1024)(128)(2,1)S(1)}, u32[]{:S(2)}, u32[]{:S(2)}) collective-permute-start(bf16[165888]{0:T(1024)(128)(2,1)} %collective-permute-done.6), channel_id=1, source_target_pairs={{0,2},{2,4},{4,6},{6,8},{8,10},{10,12},{12,14},{14,16},{16,18},{18... | collective-permute-start | bytes 995336 | tf_op jit(solution)/shard_map/ppermute | solution.py:204
  187.0 8.3 %copy-start.16 = (bf16[1,165888]{1,0:T(2,128)(2,1)S(1)}, bf16[1,165888]{1,0:T(2,128)(2,1)}, u32[]{:S(2)}) copy-start(bf16[1,165888]{1,0:T(2,128)(2,1)} %stack.58) | copy-start | bytes 995332
  187.0 8.3 %copy-start.17 = (bf16[1,165888]{1,0:T(2,128)(2,1)S(1)}, bf16[1,165888]{1,0:T(2,128)(2,1)}, u32[]{:S(2)}) copy-start(bf16[1,165888]{1,0:T(2,128)(2,1)} %stack.60) | copy-start | bytes 995332
  259.1 11.3 %copy-start.14 = (bf16[256,576]{0,1:T(8,128)(2,1)S(1)}, bf16[256,576]{0,1:T(8,128)(2,1)}, u32[]{:S(2)}) copy-start(bf16[256,576]{0,1:T(8,128)(2,1)} %multiply_convert_fusion.3) | copy-start | bytes 884740
  259.2 13.7 %copy-start.19 = (bf16[256,576]{0,1:T(8,128)(2,1)S(1)}, bf16[256,576]{0,1:T(8,128)(2,1)}, u32[]{:S(2)}) copy-start(bf16[256,576]{0,1:T(8,128)(2,1)} %param.16) | copy-start | bytes 884740
  270.5 4.8 copy-start.1
  310.2 44.7 %reduce-scatter.5.cloned.1.call-start = ((), (), s32[]{:S(2)}) async-start(), calls=%async_computation.3 | async-start | bytes 589824 | tf_op jit(solution)/shard_map/reduce_scatter | solution.py:313
  319.3 5.4 copy-start.15
  319.3 5.4 copy-start.36
  327.1 4.7 copy-start.34
  338.7 11.3 %copy-start.28 = (f32[256,64]{0,1:T(8,128)S(1)}, f32[256,64]{0,1:T(8,128)}, u32[]{:S(2)}) copy-start(f32[256,64]{0,1:T(8,128)} %copy-done.27) | copy-start | bytes 196612
  338.7 12.4 %copy-start.26 = (f32[256,64]{0,1:T(8,128)S(1)}, f32[256,64]{0,1:T(8,128)}, u32[]{:S(2)}) copy-start(f32[256,64]{0,1:T(8,128)} %copy-done.24) | copy-start | bytes 196612
  338.7 298.7 %all-reduce.13.cloned.1.call-start = ((), (), s32[]{:S(2)}) async-start(), calls=%async_computation.6 | async-start | bytes 28327936
  353.7 5.2 copy-start.10
  353.7 5.2 copy-start.45
  386.3 5.0 copy-start.3
  386.3 277.8 %all-reduce.11.cloned.1.call-start = ((), (), s32[]{:S(2)}) async-start(), calls=%async_computation.5 | async-start | bytes 450560
  391.3 262.3 %copy-start.18 = (f32[165888]{0:T(1024)S(1)}, f32[165888]{0:T(1024)}, u32[]{:S(2)}) copy-start(f32[165888]{0:T(1024)} %param.21) | copy-start | bytes 1990660
  640.6 23.4 %copy-start.31 = (f32[55368]{0:T(1024)S(1)}, f32[55368]{0:T(1024)}, u32[]{:S(2)}) copy-start(f32[55368]{0:T(1024)} %param.18) | copy-start | bytes 664420
  640.6 23.4 %copy-start.43 = (f32[55368]{0:T(1024)S(1)}, f32[55368]{0:T(1024)}, u32[]{:S(2)}) copy-start(f32[55368]{0:T(1024)} %param.19) | copy-start | bytes 664420
  640.6 23.4 %copy-start.44 = (f32[55368]{0:T(1024)S(1)}, f32[55368]{0:T(1024)}, u32[]{:S(2)}) copy-start(f32[55368]{0:T(1024)} %param.20) | copy-start | bytes 664420
  (19 other events, 41.7 us)
Sparse Core Ops, SparseCore 0:
  19.5 99.3 all-reduce.8
  310.3 14.2 reduce-scatter.2
  338.8 14.3 reduce-scatter.4
  386.4 250.9 all-reduce.12
  640.1 23.8 all-reduce.10
